TPU v7x, 32 devices: a whole 2x2x4 slice. The times are simulated.
32 devices in a mesh: grp: 4 (over y, x), space: 8 (over z, core).
Axes of the slice: x: 2, y: 2, z: 4, core: 2. Of those that a mesh axis runs over, the one named last changes fastest.
Arguments:
- features: bfloat16 [4, 128, 128, 128], P('grp', 'space'), may hold values from -6 to 6
- weights: bfloat16 [27, 128, 128], replicated, may hold values from -0.109375 to 0.109375
- cotangent: bfloat16 [4, 128, 128, 128], P('grp', 'space'), may hold values from -6 to 6
- kernel_map: int32 [4, 128, 27], P('grp', 'space'), may hold values from -1 to 127, as said below
- counts: int32 [4, 8], P('grp', 'space'), may hold values from 4 to 16
Outputs:
- output: bfloat16 [4, 128, 128, 128], P('grp', 'space')
- input_grad: bfloat16 [4, 128, 128, 128], P('grp', 'space')
- weight_grad: float32 [3456, 128], P('space')
Inputs may be any that keep to these rules, and one draw needn't show every extreme that they name: `kernel_map`: the centre offset k = 27 div 2 maps every block to itself. Otherwise an entry for an output block b on slab d = b div 16 is -1 or lies in [d * 16 - 4, (d + 1) * 16 + 4) within the sample. The live blocks of a device are its first counts slots.
All inputs are finite; a program needn't handle non-finite values.
Results may differ from a plain program's by a relative error of at most 0.005.
Values may be sent and summed in bfloat16 or wider, within the bound.
A program may use at most 64 MiB of HBM per device.

v0:
```python
import jax
import jax.numpy as jnp
from jax import lax
from jax.sharding import PartitionSpec as P

K = 27
H = 4


def extended_2(block, sides, width):
    for axis, dim in sides:
        count = lax.axis_size(axis)
        forward = [(i, i + 1) for i in range(count - 1)]
        backward = [(target, source) for source, target in forward]
        low = lax.ppermute(
            lax.slice_in_dim(block, block.shape[dim] - width, None, axis=dim), axis, forward
        )
        high = lax.ppermute(lax.slice_in_dim(block, 0, width, axis=dim), axis, backward)
        block = jnp.concatenate([low, block, high], axis=dim)
    return block


def passed_along(block, axis, distance):
    devices = range(lax.axis_size(axis))
    route = [(i - distance, i) for i in devices if i - distance in devices]
    return lax.ppermute(block, axis, route)


def per_device(features, weights, cotangent, kernel_map, counts):
    voxels = features[0]
    slots = voxels.shape[0]
    device = lax.axis_index("space")
    live_mask = (jnp.arange(slots) < counts[0, 0]).astype(jnp.bfloat16)[:, None, None]
    live_float = live_mask.astype(jnp.float32)
    masked = voxels * live_mask
    grad_out = cotangent[0] * live_mask
    extended = extended_2(masked, (("space", 0),), H)
    block_map = kernel_map[0]
    first_block = device * slots - H
    present = (block_map >= 0).astype(jnp.bfloat16)
    local_index = jnp.where(block_map >= 0, block_map - first_block, 0)
    channels_in = voxels.shape[2]
    channels_out = weights.shape[2]

    def step(offset, carry):
        total, grad_in, wgrad = carry
        column = lax.dynamic_index_in_dim(local_index, offset, 1, keepdims=False)
        present_k = lax.dynamic_index_in_dim(present, offset, 1, keepdims=False)[:, None, None]
        gathered = jnp.take(extended, column, axis=0) * present_k
        kernel = lax.dynamic_index_in_dim(weights, offset, 0, keepdims=False)
        total = total + jnp.einsum(
            "brc,co->bro", gathered, kernel, preferred_element_type=jnp.float32
        )
        term = jnp.einsum("bro,co->brc", grad_out, kernel, preferred_element_type=jnp.float32)
        grad_in = grad_in.at[column].add(term * present_k.astype(jnp.float32))
        piece = jnp.einsum("brc,bro->co", gathered, grad_out, preferred_element_type=jnp.float32)
        wgrad = lax.dynamic_update_index_in_dim(wgrad, piece, offset, 0)
        return (total, grad_in, wgrad)

    start = (
        jnp.zeros((slots, voxels.shape[1], channels_out), jnp.float32),
        jnp.zeros((slots + 2 * H, voxels.shape[1], channels_in), jnp.float32),
        jnp.zeros((K, channels_in, channels_out), jnp.float32),
    )
    total, grad_in, wgrad = lax.fori_loop(0, K, step, start)
    output = (total * live_float).astype(jnp.bfloat16)
    lower_rim = grad_in[:H]
    upper_rim = grad_in[slots + H :]
    own_grad = grad_in[H : slots + H]
    from_above = passed_along(lower_rim.astype(jnp.bfloat16), "space", -1).astype(lower_rim.dtype)
    from_below = passed_along(upper_rim.astype(jnp.bfloat16), "space", 1).astype(upper_rim.dtype)
    own_grad = own_grad.at[:H].add(from_below)
    own_grad = own_grad.at[slots - H :].add(from_above)
    input_grad = (own_grad * live_float).astype(jnp.bfloat16)
    weight_rows = wgrad.reshape(K * channels_in, channels_out)
    summed = lax.psum(weight_rows, ("grp", "space"))
    row_count = weight_rows.shape[0] // lax.axis_size("space")
    own_rows = lax.dynamic_slice_in_dim(summed, device * row_count, row_count, 0)
    return (output[None], input_grad[None], own_rows)


def solution(mesh):
    in_specs = (
        P("grp", "space", None, None),
        P(),
        P("grp", "space", None, None),
        P("grp", "space", None),
        P("grp", "space"),
    )
    out_specs = (P("grp", "space", None, None), P("grp", "space", None, None), P("space", None))
    return jax.shard_map(
        per_device, mesh=mesh, in_specs=in_specs, out_specs=out_specs, check_vma=False
    )
```

profile of v0, /device:TPU:0, one launch (start us, length us, event | category | flops | bytes accessed | tf_op | source)
XLA Modules:
  0.0 446.3 jit_solution(6604111132095993957)
XLA Ops:
  13.1 4.0 collective-permute-done.1
  19.4 278.8 %while.20 = (s32[]{:T(128)}, f32[16,128,128]{2,1,0:T(8,128)}, f32[24,128,128]{2,1,0:T(8,128)}, f32[27,128,128]{2,1,0:T(8,128)}, s32[16,27]{0,1:T(8,128)S(1)}, /*...) while((s32[]{:T(128)}, f32[16,128,128]{2,1,0:T(8,128)}, ...), condition=%wide.region_2.3_spmd.clone, body=%wide.region_0.2_spmd.clone.sunk | while | flops 203424880 | bytes 11670275 | solution.py:65
  24.7 3.3 scatter_fusion
  35.0 3.3 scatter_fusion
  41.3 2.6 convolution_add_fusion.2
  45.3 3.4 scatter_fusion
  55.7 3.4 scatter_fusion
  62.0 2.6 convolution_add_fusion.2
  66.0 3.3 scatter_fusion
  72.3 2.6 convolution_add_fusion.2
  76.3 3.3 scatter_fusion
  82.6 2.6 convolution_add_fusion.2
  86.6 3.4 scatter_fusion
  92.9 2.6 convolution_add_fusion.2
  97.0 3.4 scatter_fusion
  103.3 2.6 convolution_add_fusion.2
  107.3 3.3 scatter_fusion
  113.5 2.6 convolution_add_fusion.2
  117.6 3.6 scatter_fusion
  124.1 2.6 convolution_add_fusion.2
  128.1 3.3 scatter_fusion
  134.4 2.6 convolution_add_fusion.2
  138.4 3.4 scatter_fusion
  144.8 2.6 convolution_add_fusion.2
  148.8 3.4 scatter_fusion
  155.2 2.6 convolution_add_fusion.2
  159.2 3.4 scatter_fusion
  165.5 2.6 convolution_add_fusion.2
  169.5 3.3 scatter_fusion
  179.8 3.3 scatter_fusion
  186.1 2.6 convolution_add_fusion.2
  190.1 3.5 scatter_fusion
  196.6 2.6 convolution_add_fusion.2
  200.6 3.4 scatter_fusion
  210.9 3.5 scatter_fusion
  217.3 2.6 convolution_add_fusion.2
  221.3 3.5 scatter_fusion
  231.8 3.4 scatter_fusion
  238.2 2.6 convolution_add_fusion.2
  242.2 3.3 scatter_fusion
  252.4 3.3 scatter_fusion
  258.7 2.6 convolution_add_fusion.2
  262.7 3.3 scatter_fusion
  273.0 3.3 scatter_fusion
  283.3 3.4 scatter_fusion
  293.7 3.4 scatter_fusion
  299.9 5.3 %collective-permute-start.2 = (bf16[4,128,128]{2,1,0:T(8,128)(2,1)S(1)}, bf16[4,128,128]{2,1,0:T(8,128)(2,1)S(1)}, u32[]{:S(2)}, u32[]{:S(2)}) collective-permute-start(bf16[4,128,128]{2,1,0:T(8,128)(2,1)S(1)} %get-tuple-element.239), channel_id=1, source_target_pairs={{0,1},{1,2},{2,3},{3,4},{4,5},{5,6},{6,7},{8,9},{9,10},{10,11},{11... | collective-permute-start | bytes 393224 | tf_op jit(solution)/shard_map/ppermute | solution.py:26
  311.2 126.7 %all-reduce.2.cloned.1.call-done = f32[3456,128]{1,0:T(8,128)} async-done(((f32[3456,128]{1,0:T(8,128)}), f32[3456,128]{1,0:T(8,128)}) %all-reduce.2.cloned.1.call-update) | async-done | bytes 1769488 | tf_op jit(solution)/shard_map/psum | solution.py:76
  (229 shorter events, 158.9 us)
Async XLA Ops:
  7.2 5.8 %copy-start.1 = (s32[1,16,27]{2,1,0:T(8,128)S(1)}, s32[1,16,27]{2,1,0:T(8,128)}, u32[]{:S(2)}) copy-start(s32[1,16,27]{2,1,0:T(8,128)} %param.14) | copy-start | bytes 5188
  7.2 430.7 %all-reduce.2.cloned.1.call-start = ((), (), s32[]{:S(2)}) async-start(), calls=%async_computation | async-start | bytes 3538944 | tf_op jit(solution)/shard_map/psum | solution.py:76
  9.2 3.8 collective-permute-start
  11.7 5.4 %collective-permute-start.1 = (bf16[4,128,128]{2,1,0:T(8,128)(2,1)S(1)}, bf16[4,128,128]{2,1,0:T(8,128)(2,1)S(1)}, u32[]{:S(2)}, u32[]{:S(2)}) collective-permute-start(bf16[4,128,128]{2,1,0:T(8,128)(2,1)S(1)} %get-tuple-element.241), channel_id=1, source_target_pairs={{1,0},{2,1},{3,2},{4,3},{5,4},{6,5},{7,6},{9,8},{10,9},{11,10},{12... | collective-permute-start | bytes 393224 | tf_op jit(solution)/shard_map/ppermute | solution.py:18
  298.2 7.1 %copy-start = (f32[24,128,128]{2,1,0:T(8,128)S(1)}, f32[24,128,128]{2,1,0:T(8,128)}, u32[]{:S(2)}) copy-start(f32[24,128,128]{2,1,0:T(8,128)} %get-tuple-element.184) | copy-start | bytes 4718596
  299.9 6.7 %collective-permute-start.2 = (bf16[4,128,128]{2,1,0:T(8,128)(2,1)S(1)}, bf16[4,128,128]{2,1,0:T(8,128)(2,1)S(1)}, u32[]{:S(2)}, u32[]{:S(2)}) collective-permute-start(bf16[4,128,128]{2,1,0:T(8,128)(2,1)S(1)} %get-tuple-element.239), channel_id=1, source_target_pairs={{0,1},{1,2},{2,3},{3,4},{4,5},{5,6},{6,7},{8,9},{9,10},{10,11},{11... | collective-permute-start | bytes 393224 | tf_op jit(solution)/shard_map/ppermute | solution.py:26
  305.3 3.2 collective-permute-start.3
Sparse Core Ops, SparseCore 0:
  305.4 132.4 all-reduce.1
where the time goes:
time: 452 us; the launch traced here: 446 us
  waiting for transfers between devices  133 us (29%)
  matrix products  129 us (29%)
  other arithmetic  98.6 us (22%)
  local copies, waits for them, and re-layouts  60.2 us (13%)
  between operations  14.8 us (3%)
  starting transfers between devices  10.3 us (2%)
    psum x1, waiting for transfers between devices, per_device(): summed = lax.psum(weight_rows, ('grp', 'space'))  127 us
    scatter-add x27, other arithmetic, step(): grad_in = grad_in.at[column].add(term * present_k.astype(jnp.float32))  91.3 us
    dot_general x27, matrix products, step(): jnp.einsum('brc,co->bro', gathered, kernel, preferred_element_type=jnp.fl...  70 us
    gather x27, local copies, waits for them, and re-layouts, step(): gathered = jnp.take(extended, column, axis=0) * present_k  48.1 us
    dot_general x27, matrix products, step(): jnp.einsum('brc,bro->co', gathered, grad_out, preferred_element_type=jnp....  30.5 us
    dot_general x27, matrix products, step(): jnp.einsum('bro,co->brc', grad_out, kernel, preferred_element_type=jnp.fl...  28.4 us
  transfers between devices with their start and end apart: 5, of which 3 were waited for; matrix products, arithmetic and copies ran while one was open for 1% of the time, Pallas kernels for 0%

commit v1 on v0

v1 whole, which is shorter than its diff:
```python
import functools

import jax
import jax.numpy as jnp
from jax import lax
from jax.experimental import pallas as pl
from jax.experimental.pallas import tpu as pltpu
from jax.sharding import PartitionSpec as P

H = 4
BF16, F32 = jnp.bfloat16, jnp.float32
VMEM = pl.BlockSpec(memory_space=pltpu.VMEM)
SMEM = pl.BlockSpec(memory_space=pltpu.SMEM)


def fill_extended(ext, low, own, high, change=lambda x: x):
    slots = own.shape[0]
    for i in range(H):
        ext[i] = change(low[i])
        ext[H + slots + i] = change(high[i])
    for i in range(slots):
        ext[H + i] = change(own[i])
    ext[2 * H + slots] = jnp.zeros(ext.shape[1:], ext.dtype)


def input_grad_kernel(idx, cot, w, rims, own, acc):
    slots = cot.shape[0]
    offsets = idx.shape[1]
    cin = acc.shape[2]

    def clear(i, carry):
        acc[i] = jnp.zeros(acc.shape[1:], F32)
        return carry

    lax.fori_loop(0, acc.shape[0], clear, 0)

    def body(b, carry):
        g = cot[b]
        for k in range(0, offsets, 2):
            n = min(2, offsets - k)
            term = lax.dot_general(
                g, w[k * cin : (k + n) * cin], (((1,), (1,)), ((), ())), preferred_element_type=F32
            )
            for j in range(n):
                a = idx[b, k + j]
                acc[a] = acc[a] + term[:, j * cin : (j + 1) * cin]
        return carry

    lax.fori_loop(0, slots, body, 0)
    for i in range(H):
        rims[0, i] = acc[i].astype(BF16)
        rims[1, i] = acc[H + slots + i].astype(BF16)
    for i in range(slots):
        own[i] = acc[H + i]


def weight_grad_kernel(idx, low, feat, high, cot, part, ext):
    slots = feat.shape[0]
    offsets = idx.shape[1]
    cin = feat.shape[2]
    group = 3 if offsets % 3 == 0 else 1
    fill_extended(ext, low, feat, high, lambda x: x.T)
    def body(i, carry):
        rows = [
            jnp.concatenate([ext[idx[b, i * group + j]] for b in range(slots)], axis=1)
            for j in range(group)
        ]
        got = jnp.dot(jnp.concatenate(rows, axis=0), cot[...], preferred_element_type=F32)
        part[pl.ds(pl.multiple_of(i * group * cin, group * cin), group * cin), :] = got.astype(BF16)
        return carry

    lax.fori_loop(0, offsets // group, body, 0)


def window_start(g, groups, unit, rows):
    return pl.multiple_of(g * unit - (g // (groups - 1)) * (groups * unit - rows), 16)


def reduce_kernel(
    groups, space, unit,
    idx, live, low, feat, high, w, part, rims, own,
    out, ig, wg,
    ext, r0, p1, r1, p2, r2, r3, from_below, from_above,
    s0, q0, s1, q1, s2, q2, s3, q3, sr, qr,
):
    g = lax.axis_index("grp")
    s = lax.axis_index("space")
    half = space // 2
    z, c = s // 2, s % 2
    slots = feat.shape[0]
    offsets = idx.shape[1]
    rows = part.shape[2]
    partner = (g, z * 2 + (1 - c))
    grp_peers = [((g + d) % groups, s) for d in range(1, groups)]
    z_peers = [(g, ((z + d) % half) * 2 + c) for d in range(1, half)]

    barrier = pltpu.get_barrier_semaphore()
    fixed = [partner] + grp_peers + z_peers
    for peer in fixed:
        pl.semaphore_signal(barrier, inc=1, device_id=peer, device_id_type=pl.DeviceIdType.MESH)

    across = s - 1 + 2 * c
    has_across = jnp.logical_and(across >= 0, across < space)

    @pl.when(has_across)
    def _():
        pl.semaphore_signal(barrier, inc=1, device_id=(g, across), device_id_type=pl.DeviceIdType.MESH)

    fill_extended(ext, low, feat, high)
    pl.semaphore_wait(barrier, len(fixed) + has_across.astype(jnp.int32))

    def remote(src, dst, send, recv, peer):
        return pltpu.make_async_remote_copy(
            src_ref=src, dst_ref=dst, send_sem=send, recv_sem=recv,
            device_id=peer, device_id_type=pl.DeviceIdType.MESH,
        )

    copy0 = remote(part.at[:, 1 - c], r0, s0, q0, partner)
    copy0.start()
    down = remote(rims.at[0], from_above, sr.at[0], qr.at[0], (g, s - 1))
    up = remote(rims.at[1], from_below, sr.at[1], qr.at[1], (g, s + 1))

    @pl.when(s > 0)
    def _():
        down.start()

    @pl.when(s < space - 1)
    def _():
        up.start()

    pairs = slots // 2

    def forward(i, carry):
        rows_of = [
            jnp.concatenate([ext[idx[2 * i + j, k]] for k in range(offsets)], axis=1)
            for j in range(2)
        ]
        got = jnp.dot(jnp.concatenate(rows_of, axis=0), w[...], preferred_element_type=F32)
        n = feat.shape[1]
        for j in range(2):
            out[2 * i + j] = got[j * n : (j + 1) * n].astype(BF16)
        return carry

    def forward_part(q):
        lax.fori_loop(q * pairs // 4, (q + 1) * pairs // 4, forward, 0)

    forward_part(0)
    copy0.wait_recv()
    for i in range(half):
        p1[i] = (part[i, c].astype(F32) + r0[i].astype(F32)).astype(BF16)

    copies1 = []
    for d in range(1, groups):
        there = window_start((g + d) % groups, groups, unit, rows)
        copies1.append(
            remote(p1.at[:, pl.ds(there, unit)], r1.at[d - 1], s1.at[d - 1], q1.at[d - 1], grp_peers[d - 1])
        )
        copies1[-1].start()
    forward_part(1)
    for copy in copies1:
        copy.wait_recv()
    here = window_start(g, groups, unit, rows)
    for i in range(half):
        total = p1[i, pl.ds(here, unit), :].astype(F32)
        for d in range(1, groups):
            total = total + r1[d - 1, i].astype(F32)
        p2[i] = total.astype(BF16)

    copies2 = []
    for d in range(1, half):
        copies2.append(
            remote(p2.at[(z + d) % half], r2.at[d - 1], s2.at[d - 1], q2.at[d - 1], z_peers[d - 1])
        )
        copies2[-1].start()
    forward_part(2)
    for copy in copies2:
        copy.wait_recv()
    total = p2[z].astype(F32)
    for d in range(1, half):
        total = total + r2[d - 1].astype(F32)
    r3[0] = total

    copies3 = []
    for d in range(1, groups):
        copies3.append(remote(r3.at[0], r3.at[d], s3.at[d - 1], q3.at[d - 1], grp_peers[d - 1]))
        copies3[-1].start()
    forward_part(3)

    @pl.when(s < space - 1)
    def _():
        down.wait_recv()

    @pl.when(s > 0)
    def _():
        up.wait_recv()

    for i in range(slots):
        alive = jnp.where(i < live[0], 1.0, 0.0).astype(F32)
        value = own[i]
        if i < H:
            value = value + jnp.where(s > 0, from_below[i].astype(F32), 0.0)
        if i >= slots - H:
            value = value + jnp.where(s < space - 1, from_above[i - slots + H].astype(F32), 0.0)
        ig[i] = (value * alive).astype(BF16)

    for copy in copies3:
        copy.wait_recv()
    for j in range(groups):
        first = min(j * unit, rows - unit)
        wg[first : first + unit, :] = r3[(g - j + groups) % groups]
    copy0.wait_send()
    for copy in copies1 + copies2 + copies3:
        copy.wait_send()

    @pl.when(s > 0)
    def _():
        down.wait_send()

    @pl.when(s < space - 1)
    def _():
        up.wait_send()


def per_device(features, weights, cotangent, kernel_map, counts):
    voxels = features[0]
    slots, height, cin = voxels.shape
    offsets, _, cout = weights.shape
    space = lax.axis_size("space")
    groups = lax.axis_size("grp")
    device = lax.axis_index("space")
    live = counts[0]
    block_map = kernel_map[0]
    local = block_map - (device * slots - H)
    nowhere = slots + 2 * H
    slot_ids = jnp.arange(slots, dtype=jnp.int32)[:, None]
    usable = (block_map >= 0) & (slot_ids < live[0]) & ((local - H < live[0]) | (local >= slots + H))
    idx = jnp.where(usable, local, nowhere).astype(jnp.int32)
    high_ids = jnp.arange(slots - H, slots)
    top = voxels[slots - H :] * (high_ids < live[0]).astype(BF16)[:, None, None]
    up_route = [(i, i + 1) for i in range(space - 1)]
    low = lax.ppermute(top, "space", up_route)
    high = lax.ppermute(voxels[:H], "space", [(b, a) for a, b in up_route])
    flat_w = weights.reshape(offsets * cin, cout)

    rims, own = pl.pallas_call(
        input_grad_kernel,
        out_shape=(
            jax.ShapeDtypeStruct((2, H, height, cin), BF16),
            jax.ShapeDtypeStruct((slots, height, cin), F32),
        ),
        in_specs=[SMEM, VMEM, VMEM],
        out_specs=(VMEM, VMEM),
        scratch_shapes=[pltpu.VMEM((nowhere + 1, height, cin), F32)],
        cost_estimate=pl.CostEstimate(
            flops=2 * slots * height * cin * cout * offsets, bytes_accessed=4_000_000, transcendentals=0
        ),
        name="input_grad",
    )(idx, cotangent[0], flat_w)

    part = pl.pallas_call(
        weight_grad_kernel,
        out_shape=jax.ShapeDtypeStruct((offsets * cin, cout), BF16),
        in_specs=[SMEM] + [VMEM] * 4,
        out_specs=VMEM,
        scratch_shapes=[pltpu.VMEM((nowhere + 1, cin, height), BF16)],
        cost_estimate=pl.CostEstimate(
            flops=2 * slots * height * cin * cout * offsets, bytes_accessed=4_000_000, transcendentals=0
        ),
        name="weight_grad",
    )(idx, low, voxels, high, cotangent[0].reshape(slots * height, cout))

    half = space // 2
    rows = offsets * cin // space
    padded = -(-rows // 16) * 16
    part = part.reshape(space, rows, cout)
    if padded != rows:
        part = jnp.pad(part, ((0, 0), (0, padded - rows), (0, 0)))
    part = part.reshape(half, 2, padded, cout)
    unit = -(-padded // (16 * groups)) * 16
    dma = pltpu.SemaphoreType.DMA
    output, input_grad, wg = pl.pallas_call(
        functools.partial(reduce_kernel, groups, space, unit),
        out_shape=(
            jax.ShapeDtypeStruct((slots, height, cout), BF16),
            jax.ShapeDtypeStruct((slots, height, cin), BF16),
            jax.ShapeDtypeStruct((padded, cout), F32),
        ),
        in_specs=[SMEM, SMEM] + [VMEM] * 7,
        out_specs=(VMEM, VMEM, VMEM),
        scratch_shapes=[
            pltpu.VMEM((nowhere + 1, height, cin), BF16),
            pltpu.VMEM((half, padded, cout), BF16),
            pltpu.VMEM((half, padded, cout), BF16),
            pltpu.VMEM((groups - 1, half, unit, cout), BF16),
            pltpu.VMEM((half, unit, cout), BF16),
            pltpu.VMEM((half - 1, unit, cout), BF16),
            pltpu.VMEM((groups, unit, cout), F32),
            pltpu.VMEM((H, height, cin), BF16),
            pltpu.VMEM((H, height, cin), BF16),
            dma, dma,
            dma((groups - 1,)), dma((groups - 1,)),
            dma((half - 1,)), dma((half - 1,)),
            dma((groups - 1,)), dma((groups - 1,)),
            dma((2,)), dma((2,)),
        ],
        compiler_params=pltpu.CompilerParams(collective_id=0, has_side_effects=True),
        name="reduce_forward",
    )(idx, live, low, voxels, high, flat_w, part, rims, own)
    return output[None], input_grad[None], wg[:rows]


def solution(mesh):
    in_specs = (
        P("grp", "space", None, None),
        P(),
        P("grp", "space", None, None),
        P("grp", "space", None),
        P("grp", "space"),
    )
    out_specs = (P("grp", "space", None, None), P("grp", "space", None, None), P("space", None))
    return jax.shard_map(
        per_device, mesh=mesh, in_specs=in_specs, out_specs=out_specs, check_vma=False
    )
```

time: 452 us -> 55.9 us (0.12); the launches traced: 446 us -> 55.6 us
  waiting for transfers between devices: 133 us -> 0.01 us
  matrix products: 129 us -> 0 us
  other arithmetic: 98.6 us -> 1.67 us
  local copies, waits for them, and re-layouts: 60.2 us -> 5.36 us
  Pallas kernels: 0 us -> 42.9 us
  between operations: 14.8 us -> 1.37 us
  starting transfers between devices: 10.3 us -> 4.33 us
    dot_general x81 -> x0, matrix products: 129 us -> none  [the longest x27 70 us: step(): jnp.einsum('brc,co->bro', gathered, kernel, preferred_element_type=jnp.fl...]
    psum x1 -> x0, waiting for transfers between devices: 127 us -> none  [per_device(): summed = lax.psum(weight_rows, ('grp', 'space'))]
    scatter-add x29 -> x0, other arithmetic: 91.4 us -> none  [the longest x27 91.3 us: step(): grad_in = grad_in.at[column].add(term * present_k.astype(jnp.float32))]
    gather x27 -> x0, local copies, waits for them, and re-layouts: 48.1 us -> none  [step(): gathered = jnp.take(extended, column, axis=0) * present_k]
    pallas_call x0 -> x3, Pallas kernels: none -> 42.9 us  [the longest x1 25.9 us: per_device(): pl.pallas_call(functools.partial(reduce_kernel, groups, space, unit), out...]
    mul x27 -> x0, local copies, waits for them, and re-layouts: 8.94 us -> none  [step(): grad_in = grad_in.at[column].add(term * present_k.astype(jnp.float32))]
    ppermute x4 -> x2, starting transfers between devices: 10.3 us -> 4.33 us  [the longest x1 3.04 us: per_device(): low = lax.ppermute(top, 'space', up_route)]
    ppermute x4 -> x2, waiting for transfers between devices: 5.87 us -> 0.01 us  [the longest x1 0.01 us: per_device(): high = lax.ppermute(voxels[:H], 'space', [(b, a) for a, b in up_route])]
  transfers between devices with their start and end apart: 5 -> 2, of which waited for: 3 -> 0; matrix products, arithmetic and copies ran while one was open for 1% -> 3% of each run, Pallas kernels for 0% -> 17%
where the time goes in v1:
time: 55.9 us; the launch traced here: 55.6 us
  Pallas kernels  42.9 us (77%)
  local copies, waits for them, and re-layouts  5.36 us (10%)
  starting transfers between devices  4.33 us (8%)
  other arithmetic  1.67 us (3%)
  between operations  1.37 us (2%)
    pallas_call x1, Pallas kernels, per_device(): pl.pallas_call(functools.partial(reduce_kernel, groups, space, unit), out...  25.9 us
    pallas_call x1, Pallas kernels, per_device(): pl.pallas_call(input_grad_kernel, out_shape=(jax.ShapeDtypeStruct((2, H,...  9.28 us
    pallas_call x1, Pallas kernels, per_device(): pl.pallas_call(weight_grad_kernel, out_shape=jax.ShapeDtypeStruct((offset...  7.69 us
    unnamed x13, local copies, waits for them, and re-layouts  4.45 us
    ppermute x1, starting transfers between devices, per_device(): low = lax.ppermute(top, 'space', up_route)  3.04 us
    ppermute x1, starting transfers between devices, per_device(): high = lax.ppermute(voxels[:H], 'space', [(b, a) for a, b in up_route])  1.29 us
  transfers between devices with their start and end apart: 2, of which 0 were waited for; matrix products, arithmetic and copies ran while one was open for 3% of the time, Pallas kernels for 17%

profile of v1, /device:TPU:0, one launch (start us, length us, event | category | flops | bytes accessed | tf_op | source)
XLA Modules:
  0.0 55.6 jit_solution(8648785275844638319)
XLA Ops:
  0.6 0.9 %slice_bitcast_fusion = bf16[4,128,128]{2,1,0:T(8,128)(2,1)S(1)} fusion(bf16[1,16,128,128]{3,2,1,0:T(8,128)(2,1)} %param.5), kind=kLoop, calls=%fused_computation.1 | loop fusion | bytes 262144 | tf_op jit(solution)/shard_map/slice | solution.py:242
  1.5 1.3 %collective-permute-start.1 = (bf16[4,128,128]{2,1,0:T(8,128)(2,1)S(1)}, bf16[4,128,128]{2,1,0:T(8,128)(2,1)S(1)}, u32[]{:S(2)}, u32[]{:S(2)}) collective-permute-start(bf16[4,128,128]{2,1,0:T(8,128)(2,1)S(1)} %slice_bitcast_fusion), channel_id=1, source_target_pairs={{1,0},{2,1},{3,2},{4,3},{5,4},{6,5},{7,6},{9,8},{10,9},{11,10},{12... | collective-permute-start | bytes 393224 | tf_op jit(solution)/shard_map/ppermute | solution.py:242
  3.5 1.0 %bitcast_multiply_fusion = bf16[4,128,128]{2,1,0:T(8,128)(2,1)S(1)} fusion(bf16[1,16,128,128]{3,2,1,0:T(8,128)(2,1)} %param.5, bf16[4]{0:T(256)(128)(2,1)S(1)} %compare_convert_fusion), kind=kLoop, calls=%fused_computation | loop fusion | flops 65536 | bytes 262152 | tf_op jit(solution)/shard_map/mul | solution.py:239
  4.5 0.0 copy-start.4
  4.5 3.0 %collective-permute-start = (bf16[4,128,128]{2,1,0:T(8,128)(2,1)S(1)}, bf16[4,128,128]{2,1,0:T(8,128)(2,1)S(1)}, u32[]{:S(2)}, u32[]{:S(2)}) collective-permute-start(bf16[4,128,128]{2,1,0:T(8,128)(2,1)S(1)} %bitcast_multiply_fusion), channel_id=1, source_target_pairs={{0,1},{1,2},{2,3},{3,4},{4,5},{5,6},{6,7},{8,9},{9,10},{10,11},{11... | collective-permute-start | bytes 393224 | tf_op jit(solution)/shard_map/ppermute | solution.py:241
  7.6 0.0 copy-done.4
  7.6 0.7 %bitcast_select_fusion.idx = s32[16,27]{1,0:T(8,128)} fusion(s32[1,16,27]{2,1,0:T(8,128)S(1)} %copy-done.4, s32[]{:T(128)} %bitcast.32, s32[]{:T(128)S(6)} %sub.16, pred[16]{0:T(512)(128)(4,1)S(1)} %iota_compare_fusion), kind=kLoop, calls=%fused_computation.2 | loop fusion | flops 3888 | bytes 3480 | tf_op jit(solution)/shard_map/jit(_where)/select_n | solution.py:237
  8.3 9.3 %input_grad.1 = (bf16[2,4,128,128]{3,2,1,0:T(8,128)(2,1)}, f32[16,128,128]{2,1,0:T(8,128)}) custom-call(s32[16,27]{1,0:T(8,128)} %bitcast_select_fusion.idx, bf16[16,128,128]{2,1,0:T(8,128)(2,1)} %bitcast.42, bf16[3456,128]{1,0:T(8,128)(2,1)} %bitcast.37), custom_call_target="tpu_custom_call" | custom-call | flops 1811939328 | bytes 4000000 | tf_op jit(solution)/shard_map/input_grad/pallas_call | solution.py:245
  17.5 0.0 collective-permute-done.1.high
  17.5 0.0 copy-start.2
  17.5 0.0 collective-permute-done.low
  17.6 0.0 copy-start.3
  17.6 0.6 %copy-done.2 = bf16[4,128,128]{2,1,0:T(8,128)(2,1)} copy-done((bf16[4,128,128]{2,1,0:T(8,128)(2,1)}, bf16[4,128,128]{2,1,0:T(8,128)(2,1)S(1)}, u32[]{:S(2)}) %copy-start.2) | copy-done | bytes 131096
  18.2 0.0 copy-done.3
  18.2 7.7 %weight_grad.1 = bf16[3456,128]{1,0:T(8,128)(2,1)} custom-call(s32[16,27]{1,0:T(8,128)} %bitcast_select_fusion.idx, bf16[4,128,128]{2,1,0:T(8,128)(2,1)} %copy-done.3, bf16[16,128,128]{2,1,0:T(8,128)(2,1)} %bitcast.35, bf16[4,128,128]{2,1,0:T(8,128)(2,1)} %copy-done.2, bf16[2048,128]{1,0:T(8,128)(2,1)} %bitcast.43), custom_call_target="tpu_custom_call" | custom-call | flops 1811939328 | bytes 4000000 | tf_op jit(solution)/shard_map/weight_grad/pallas_call | solution.py:260
  25.9 25.9 %reduce_forward.1 = (bf16[16,128,128]{2,1,0:T(8,128)(2,1)}, bf16[16,128,128]{2,1,0:T(8,128)(2,1)}, f32[432,128]{1,0:T(8,128)}) custom-call(s32[16,27]{1,0:T(8,128)} %bitcast_select_fusion.idx, s32[1]{0:T(128)} %bitcast.34.live, bf16[4,128,128]{2,1,0:T(8,128)(2,1)} %copy-done.3, bf16[16,128,128]{2,1,0:T(8,128)(2,1)} %bitcast.36, ...), custom_call_target="tpu_custom_call" | custom-call | tf_op jit(solution)/shard_map/reduce_forward/pallas_call | solution.py:281
  51.8 0.0 copy-start
  51.8 1.9 %copy.12 = bf16[1,16,128,128]{3,2,1,0:T(8,128)(2,1)} copy(bf16[1,16,128,128]{3,2,1,0:T(8,128)(2,1)} %bitcast.41) | data formatting | bytes 1048576
  53.8 0.0 copy-done
  53.8 0.0 copy-start.1
  53.8 0.8 %copy.13 = bf16[1,16,128,128]{3,2,1,0:T(8,128)(2,1)} copy(bf16[1,16,128,128]{3,2,1,0:T(8,128)(2,1)S(1)} %bitcast.40) | data formatting | bytes 1048576
  54.6 0.3 copy-done.1
  54.9 0.7 %copy.14 = f32[432,128]{1,0:T(8,128)} copy(f32[432,128]{1,0:T(8,128)S(1)} %copy-done.1) | data formatting | bytes 442368
  (2 shorter events, 0.0 us)
Async XLA Ops:
  1.5 16.0 %collective-permute-start.1 = (bf16[4,128,128]{2,1,0:T(8,128)(2,1)S(1)}, bf16[4,128,128]{2,1,0:T(8,128)(2,1)S(1)}, u32[]{:S(2)}, u32[]{:S(2)}) collective-permute-start(bf16[4,128,128]{2,1,0:T(8,128)(2,1)S(1)} %slice_bitcast_fusion), channel_id=1, source_target_pairs={{1,0},{2,1},{3,2},{4,3},{5,4},{6,5},{7,6},{9,8},{10,9},{11,10},{12... | collective-permute-start | bytes 393224 | tf_op jit(solution)/shard_map/ppermute | solution.py:242
  4.5 3.1 %copy-start.4 = (s32[1,16,27]{2,1,0:T(8,128)S(1)}, s32[1,16,27]{2,1,0:T(8,128)}, u32[]{:S(2)}) copy-start(s32[1,16,27]{2,1,0:T(8,128)} %param.8) | copy-start | bytes 5188
  4.5 13.0 %collective-permute-start = (bf16[4,128,128]{2,1,0:T(8,128)(2,1)S(1)}, bf16[4,128,128]{2,1,0:T(8,128)(2,1)S(1)}, u32[]{:S(2)}, u32[]{:S(2)}) collective-permute-start(bf16[4,128,128]{2,1,0:T(8,128)(2,1)S(1)} %bitcast_multiply_fusion), channel_id=1, source_target_pairs={{0,1},{1,2},{2,3},{3,4},{4,5},{5,6},{6,7},{8,9},{9,10},{10,11},{11... | collective-permute-start | bytes 393224 | tf_op jit(solution)/shard_map/ppermute | solution.py:241
  17.5 0.7 %copy-start.2 = (bf16[4,128,128]{2,1,0:T(8,128)(2,1)}, bf16[4,128,128]{2,1,0:T(8,128)(2,1)S(1)}, u32[]{:S(2)}) copy-start(bf16[4,128,128]{2,1,0:T(8,128)(2,1)S(1)} %collective-permute-done.1.high) | copy-start | bytes 393220
  17.6 0.7 %copy-start.3 = (bf16[4,128,128]{2,1,0:T(8,128)(2,1)}, bf16[4,128,128]{2,1,0:T(8,128)(2,1)S(1)}, u32[]{:S(2)}) copy-start(bf16[4,128,128]{2,1,0:T(8,128)(2,1)S(1)} %collective-permute-done.low) | copy-start | bytes 393220
  51.8 2.0 %copy-start = (bf16[16,128,128]{2,1,0:T(8,128)(2,1)S(1)}, bf16[16,128,128]{2,1,0:T(8,128)(2,1)}, u32[]{:S(2)}) copy-start(bf16[16,128,128]{2,1,0:T(8,128)(2,1)} %get-tuple-element.11) | copy-start | bytes 1572868
  53.8 1.1 %copy-start.1 = (f32[432,128]{1,0:T(8,128)S(1)}, f32[432,128]{1,0:T(8,128)}, u32[]{:S(2)}) copy-start(f32[432,128]{1,0:T(8,128)} %get-tuple-element.18) | copy-start | bytes 663556

commit v2 on v1

v2 whole, which is shorter than its diff:
```python
import functools

import jax
import jax.numpy as jnp
from jax import lax
from jax.experimental import pallas as pl
from jax.experimental.pallas import tpu as pltpu
from jax.sharding import PartitionSpec as P

H = 4
BF16, F32 = jnp.bfloat16, jnp.float32
VMEM = pl.BlockSpec(memory_space=pltpu.VMEM)
SMEM = pl.BlockSpec(memory_space=pltpu.SMEM)


def input_grad_kernel(where, counts, block_map, cot, feat, w, idx, top, rims, own, acc):
    slots = cot.shape[0]
    offsets = block_map.shape[1]
    cin = acc.shape[2]
    live = counts[0, 0]
    first = where[0] * slots - H
    nowhere = slots + 2 * H

    def clear(i, carry):
        acc[i] = jnp.zeros(acc.shape[1:], F32)
        return carry

    lax.fori_loop(0, acc.shape[0], clear, 0)

    def body(b, carry):
        g = cot[b]
        for k in range(0, offsets, 2):
            n = min(2, offsets - k)
            term = lax.dot_general(
                g, w[k * cin : (k + n) * cin], (((1,), (1,)), ((), ())), preferred_element_type=F32
            )
            for j in range(n):
                source = block_map[b, k + j]
                local = source - first
                dead = jnp.logical_and(local - H >= live, local < slots + H)
                skip = jnp.logical_or(jnp.logical_or(source < 0, b >= live), dead)
                a = jnp.where(skip, nowhere, local)
                idx[b, k + j] = a
                acc[a] = acc[a] + term[:, j * cin : (j + 1) * cin]
        return carry

    lax.fori_loop(0, slots, body, 0)
    for i in range(H):
        alive = jnp.where(slots - H + i < live, 1.0, 0.0).astype(BF16)
        top[i] = feat[slots - H + i] * alive
        rims[0, i] = acc[i].astype(BF16)
        rims[1, i] = acc[H + slots + i].astype(BF16)
    for i in range(slots):
        own[i] = acc[H + i]


def window_start(g, groups, unit, rows):
    return pl.multiple_of(g * unit - (g // (groups - 1)) * (groups * unit - rows), 16)


def main_kernel(
    groups, space, unit, rows, padded,
    idx, top, feat, w, cot, rims,
    out, below, above, wg,
    low, high, ext, turned, flat, part, r0, p1, r1, p2, r2, r3,
    sh, qh, sr, qr, s0, q0, s1, q1, s2, q2, s3, q3,
):
    g = lax.axis_index("grp")
    s = lax.axis_index("space")
    half = space // 2
    z, c = s // 2, s % 2
    slots, height, cin = feat.shape
    offsets = idx.shape[1]
    partner = (g, z * 2 + (1 - c))
    grp_peers = [((g + d) % groups, s) for d in range(1, groups)]
    z_peers = [(g, ((z + d) % half) * 2 + c) for d in range(1, half)]

    barrier = pltpu.get_barrier_semaphore()
    fixed = [partner] + grp_peers + z_peers
    for peer in fixed:
        pl.semaphore_signal(barrier, inc=1, device_id=peer, device_id_type=pl.DeviceIdType.MESH)
    across = s - 1 + 2 * c
    has_across = jnp.logical_and(across >= 0, across < space)

    @pl.when(has_across)
    def _():
        pl.semaphore_signal(barrier, inc=1, device_id=(g, across), device_id_type=pl.DeviceIdType.MESH)

    def place(i, block):
        ext[i] = block
        turned[i] = block.T

    for i in range(slots):
        place(H + i, feat[i])
    zero = jnp.zeros((height, cin), BF16)
    for i in [2 * H + slots]:
        place(i, zero)
    pl.semaphore_wait(barrier, len(fixed) + has_across.astype(jnp.int32))

    def remote(src, dst, send, recv, peer):
        return pltpu.make_async_remote_copy(
            src_ref=src, dst_ref=dst, send_sem=send, recv_sem=recv,
            device_id=peer, device_id_type=pl.DeviceIdType.MESH,
        )

    halo_down = remote(feat.at[pl.ds(0, H)], high, sh.at[0], qh.at[0], (g, s - 1))
    halo_up = remote(top, low, sh.at[1], qh.at[1], (g, s + 1))
    down = remote(rims.at[0], above, sr.at[0], qr.at[0], (g, s - 1))
    up = remote(rims.at[1], below, sr.at[1], qr.at[1], (g, s + 1))
    has_down, has_up = s > 0, s < space - 1

    @pl.when(has_down)
    def _():
        halo_down.start()

    @pl.when(has_up)
    def _():
        halo_up.start()

    @pl.when(has_down)
    def _():
        down.start()

    @pl.when(has_up)
    def _():
        up.start()

    @pl.when(has_down)
    def _():
        halo_up.wait_recv()
        for i in range(H):
            place(i, low[i])

    @pl.when(jnp.logical_not(has_down))
    def _():
        for i in range(H):
            place(i, zero)

    @pl.when(has_up)
    def _():
        halo_down.wait_recv()
        for i in range(H):
            place(H + slots + i, high[i])

    @pl.when(jnp.logical_not(has_up))
    def _():
        for i in range(H):
            place(H + slots + i, zero)

    group = 3 if offsets % 3 == 0 else 1
    steps = offsets // group
    span = group * cin
    direct = rows == padded

    def weight_step(i, carry):
        lhs = [
            jnp.concatenate([turned[idx[b, i * group + j]] for b in range(slots)], axis=1)
            for j in range(group)
        ]
        got = jnp.dot(jnp.concatenate(lhs, axis=0), cot[...], preferred_element_type=F32)
        at = pl.ds(pl.multiple_of(i * span, span), span)
        if direct:
            part[at, :] = got.astype(BF16)
        else:
            flat[at, :] = got
        return carry

    pairs = slots // 2

    def forward(i, carry):
        lhs = [
            jnp.concatenate([ext[idx[2 * i + j, k]] for k in range(offsets)], axis=1)
            for j in range(2)
        ]
        got = jnp.dot(jnp.concatenate(lhs, axis=0), w[...], preferred_element_type=F32)
        for j in range(2):
            out[2 * i + j] = got[j * height : (j + 1) * height].astype(BF16)
        return carry

    def piece(p):
        return pl.ds(pl.multiple_of(p * padded, 16), padded)

    done = 0
    if not direct:
        lax.fori_loop(0, steps, weight_step, 0)
        done = steps
        for p in range(space):
            part[p * padded : p * padded + rows, :] = flat[p * rows : (p + 1) * rows, :].astype(BF16)
            part[p * padded + rows : (p + 1) * padded, :] = jnp.zeros((padded - rows, part.shape[1]), BF16)

    here = window_start(g, groups, unit, padded)
    copies0, copies1 = [], []
    copies2, copies3 = [], []
    for t in range(half + 4):
        if t < half:
            need = max(done, -(-(t + 1) * 2 * rows // span))
            if need > done:
                lax.fori_loop(done, need, weight_step, 0)
                done = need
            copies0.append(remote(part.at[piece(2 * t + 1 - c)], r0.at[t], s0.at[t], q0.at[t], partner))
            copies0[t].start()
        else:
            q = t - half
            lax.fori_loop(q * pairs // 4, (q + 1) * pairs // 4, forward, 0)
        i = t - 1
        if 0 <= i < half:
            copies0[i].wait_recv()
            p1[i] = (part[piece(2 * i + c), :].astype(F32) + r0[i].astype(F32)).astype(BF16)
            copies1.append([])
            for d in range(1, groups):
                there = window_start((g + d) % groups, groups, unit, padded)
                copies1[i].append(
                    remote(p1.at[i, pl.ds(there, unit)], r1.at[i, d - 1], s1.at[i, d - 1], q1.at[i, d - 1], grp_peers[d - 1])
                )
                copies1[i][-1].start()
        i = t - 2
        if 0 <= i < half:
            total = p1[i, pl.ds(here, unit), :].astype(F32)
            for d in range(1, groups):
                copies1[i][d - 1].wait_recv()
                total = total + r1[i, d - 1].astype(F32)
            p2[i] = total.astype(BF16)
            copies2.append(remote(p2.at[i], r2.at[z], s2.at[i], q2.at[z], (g, 2 * i + c)))

            @pl.when(z != i)
            def _(i=i):
                copies2[i].start()

        if t == half + 2:
            r2[z] = p2[z]
            total = jnp.zeros((unit, wg.shape[1]), F32)
            for i in range(half):

                @pl.when(z != i)
                def _(i=i):
                    remote(p2.at[i], r2.at[i], s2.at[i], q2.at[i], (g, 2 * i + c)).wait_recv()

            for i in range(half):
                total = total + r2[i].astype(F32)
            r3[0] = total
            for d in range(1, groups):
                copies3.append(remote(r3.at[0], r3.at[d], s3.at[d - 1], q3.at[d - 1], grp_peers[d - 1]))
                copies3[-1].start()

    for copy in copies3:
        copy.wait_recv()
    for j in range(groups):
        at = min(j * unit, padded - unit)
        wg[at : at + unit, :] = r3[(g - j + groups) % groups]

    @pl.when(has_down)
    def _():
        up.wait_recv()
        halo_down.wait_send()
        down.wait_send()

    @pl.when(has_up)
    def _():
        down.wait_recv()
        halo_up.wait_send()
        up.wait_send()

    for copy in copies0 + sum(copies1, []) + copies3:
        copy.wait_send()
    for i in range(half):

        @pl.when(z != i)
        def _(i=i):
            copies2[i].wait_send()


def per_device(features, weights, cotangent, kernel_map, counts):
    voxels = features[0]
    slots, height, cin = voxels.shape
    offsets, _, cout = weights.shape
    space = lax.axis_size("space")
    groups = lax.axis_size("grp")
    device = lax.axis_index("space")
    nowhere = slots + 2 * H
    flat_w = weights.reshape(offsets * cin, cout)

    idx, top, rims, own = pl.pallas_call(
        input_grad_kernel,
        out_shape=(
            jax.ShapeDtypeStruct((slots, offsets), jnp.int32),
            jax.ShapeDtypeStruct((H, height, cin), BF16),
            jax.ShapeDtypeStruct((2, H, height, cin), BF16),
            jax.ShapeDtypeStruct((slots, height, cin), F32),
        ),
        in_specs=[SMEM, SMEM, SMEM, VMEM, VMEM, VMEM],
        out_specs=(SMEM, VMEM, VMEM, VMEM),
        scratch_shapes=[pltpu.VMEM((nowhere + 1, height, cin), F32)],
        name="input_grad",
    )(device.astype(jnp.int32).reshape(1), counts, kernel_map[0], cotangent[0], voxels, flat_w)

    half = space // 2
    rows = offsets * cin // space
    padded = -(-rows // 16) * 16
    unit = -(-padded // (16 * groups)) * 16
    dma = pltpu.SemaphoreType.DMA
    rim = jax.ShapeDtypeStruct((H, height, cin), BF16)
    output, below, above, wg = pl.pallas_call(
        functools.partial(main_kernel, groups, space, unit, rows, padded),
        out_shape=(
            jax.ShapeDtypeStruct((slots, height, cout), BF16),
            rim,
            rim,
            jax.ShapeDtypeStruct((padded, cout), F32),
        ),
        in_specs=[SMEM] + [VMEM] * 5,
        out_specs=(VMEM,) * 4,
        scratch_shapes=[
            pltpu.VMEM((H, height, cin), BF16),
            pltpu.VMEM((H, height, cin), BF16),
            pltpu.VMEM((nowhere + 1, height, cin), BF16),
            pltpu.VMEM((nowhere + 1, cin, height), BF16),
            pltpu.VMEM((offsets * cin if rows != padded else 8, cout), F32),
            pltpu.VMEM((space * padded, cout), BF16),
            pltpu.VMEM((half, padded, cout), BF16),
            pltpu.VMEM((half, padded, cout), BF16),
            pltpu.VMEM((half, groups - 1, unit, cout), BF16),
            pltpu.VMEM((half, unit, cout), BF16),
            pltpu.VMEM((half, unit, cout), BF16),
            pltpu.VMEM((groups, unit, cout), F32),
            dma((2,)), dma((2,)),
            dma((2,)), dma((2,)),
            dma((half,)), dma((half,)),
            dma((half, groups - 1)), dma((half, groups - 1)),
            dma((half,)), dma((half,)),
            dma((groups - 1,)), dma((groups - 1,)),
        ],
        compiler_params=pltpu.CompilerParams(collective_id=0, has_side_effects=True),
        name="main",
    )(idx, top, voxels, flat_w, cotangent[0].reshape(slots * height, cout), rims)
    alive = (jnp.arange(slots) < counts[0, 0])[:, None, None]
    output = output * alive.astype(BF16)
    below = jnp.where(device > 0, below.astype(F32), 0.0)
    above = jnp.where(device < space - 1, above.astype(F32), 0.0)
    gap = jnp.zeros((slots - H, height, cin), F32)
    own = own + jnp.concatenate([below, gap], axis=0) + jnp.concatenate([gap, above], axis=0)
    input_grad = (own * alive.astype(F32)).astype(BF16)
    return output[None], input_grad[None], wg[:rows]


def solution(mesh):
    in_specs = (
        P("grp", "space", None, None),
        P(),
        P("grp", "space", None, None),
        P("grp", "space", None),
        P("grp", "space"),
    )
    out_specs = (P("grp", "space", None, None), P("grp", "space", None, None), P("space", None))
    return jax.shard_map(
        per_device, mesh=mesh, in_specs=in_specs, out_specs=out_specs, check_vma=False
    )
```

time: 55.9 us -> 45.7 us (0.82)
  local copies, waits for them, and re-layouts: 5.36 us -> 0.69 us
  starting transfers between devices: 4.33 us -> 0 us
  Pallas kernels: 42.9 us -> 39.4 us
  other arithmetic: 1.67 us -> 3.99 us
    ppermute x2 -> x0, starting transfers between devices: 4.33 us -> none  [the longest x1 3.04 us: per_device(): low = lax.ppermute(top, 'space', up_route)]
    unnamed x13 -> x5, local copies, waits for them, and re-layouts: 4.45 us -> 0.69 us
    pallas_call x3 -> x2, Pallas kernels: 42.9 us -> 39.4 us  [the longest x1 29.8 us: per_device(): pl.pallas_call(functools.partial(main_kernel, groups, space, unit, rows,...]
    broadcast_in_dim x0 -> x2, other arithmetic: none -> 2.98 us  [per_device(): return (output[None], input_grad[None], wg[:rows])]
    mul x1 -> x0, other arithmetic: 0.99 us -> none  [per_device(): top = voxels[slots - H:] * (high_ids < live[0]).astype(BF16)[:, None, None]]
    slice x1 -> x0, local copies, waits for them, and re-layouts: 0.92 us -> none  [per_device(): high = lax.ppermute(voxels[:H], 'space', [(b, a) for a, b in up_route])]
  transfers between devices with their start and end apart: 2 -> 0, of which waited for: 0 -> 0; matrix products, arithmetic and copies ran while one was open for 3% -> 0% of each run, Pallas kernels for 17% -> 0%
where the time goes in v2:
time: 45.7 us; the launch traced here: 45.4 us
  Pallas kernels  39.4 us (86%)
  other arithmetic  3.99 us (9%)
  between operations  1.34 us (3%)
  local copies, waits for them, and re-layouts  0.69 us (2%)
    pallas_call x1, Pallas kernels, per_device(): pl.pallas_call(functools.partial(main_kernel, groups, space, unit, rows,...  29.8 us
    pallas_call x1, Pallas kernels, per_device(): pl.pallas_call(input_grad_kernel, out_shape=(jax.ShapeDtypeStruct((slots,...  9.61 us
    broadcast_in_dim x2, other arithmetic, per_device(): return (output[None], input_grad[None], wg[:rows])  2.98 us
    select_n x1, other arithmetic, per_device(): above = jnp.where(device < space - 1, above.astype(F32), 0.0)  1 us

profile of v2, /device:TPU:0, one launch (start us, length us, event | category | flops | bytes accessed | tf_op | source)
XLA Modules:
  0.0 45.4 jit_solution(14671196245160888378)
XLA Ops:
  1.3 9.6 %input_grad.1 = (s32[16,27]{1,0:T(8,128)}, bf16[4,128,128]{2,1,0:T(8,128)(2,1)}, bf16[2,4,128,128]{3,2,1,0:T(8,128)(2,1)}, f32[16,128,128]{2,1,0:T(8,128)}) custom-call(s32[1]{0:T(128)} %bitcast.where, s32[1,1]{1,0:T(1,128)} %copy.9.counts, s32[16,27]{1,0:T(8,128)} %bitcast.18, bf16[16,128,128]{2,1,0:T(8,128)(2,1)} %bitcast.14, ...), custom_call_target="tpu_custom_call" | custom-call | tf_op jit(solution)/shard_map/input_grad/pallas_call | solution.py:282
  10.9 29.8 %main.1 = (bf16[16,128,128]{2,1,0:T(8,128)(2,1)}, bf16[4,128,128]{2,1,0:T(8,128)(2,1)}, bf16[4,128,128]{2,1,0:T(8,128)(2,1)}, f32[432,128]{1,0:T(8,128)}) custom-call(s32[16,27]{1,0:T(8,128)} %get-tuple-element.11.idx, bf16[4,128,128]{2,1,0:T(8,128)(2,1)} %get-tuple-element.12.top, bf16[16,128,128]{2,1,0:T(8,128)(2,1)} %bitcast.17, ...), custom_call_target="tpu_custom_call" | custom-call | tf_op jit(solution)/shard_map/main/pallas_call | solution.py:302
  40.7 0.0 copy-start
  40.7 2.0 %multiply_bitcast_fusion = bf16[1,16,128,128]{3,2,1,0:T(8,128)(2,1)} fusion(bf16[16,128,128]{2,1,0:T(8,128)(2,1)} %get-tuple-element.14, bf16[16]{0:T(256)(128)(2,1)S(1)} %get-tuple-element.22), kind=kLoop, calls=%fused_computation.2 | loop fusion | flops 262144 | bytes 1048608 | tf_op jit(solution)/shard_map/broadcast_in_dim | solution.py:342
  42.8 1.0 %convert_select_fusion = (f32[4,128,128]{2,1,0:T(8,128)S(1)}, f32[4,128,128]{2,1,0:T(8,128)S(1)}) fusion(bf16[4,128,128]{2,1,0:T(8,128)(2,1)} %get-tuple-element.17, pred[]{:T(512)S(6)} %lt.18, bf16[4,128,128]{2,1,0:T(8,128)(2,1)} %get-tuple-element.16, pred[]{:T(512)S(6)} %gt.3), kind=kLoop, calls=%fused_computation.3 | loop fusion | flops 262144 | bytes 786434 | tf_op jit(solution)/shard_map/jit(_where)/select_n | solution.py:338
  43.8 0.0 copy-done
  43.8 0.0 copy-start.1
  43.8 0.9 %fusion = bf16[1,16,128,128]{3,2,1,0:T(8,128)(2,1)} fusion(f32[4,128,128]{2,1,0:T(8,128)S(1)} %get-tuple-element.19, f32[16,128,128]{2,1,0:T(8,128)S(1)} %copy-done, f32[4,128,128]{2,1,0:T(8,128)S(1)} %get-tuple-element.20, f32[16]{0:T(128)S(1)} %get-tuple-element.21), kind=kLoop, calls=%fused_computation.1 | loop fusion | flops 1048576 | bytes 2097216 | tf_op jit(solution)/shard_map/broadcast_in_dim | solution.py:342
  44.7 0.0 copy-done.1
  44.7 0.7 %copy.10 = f32[432,128]{1,0:T(8,128)} copy(f32[432,128]{1,0:T(8,128)S(1)} %copy-done.1) | data formatting | bytes 442368
  (1 shorter events, 0.0 us)
Async XLA Ops:
  40.7 3.0 %copy-start = (f32[16,128,128]{2,1,0:T(8,128)S(1)}, f32[16,128,128]{2,1,0:T(8,128)}, u32[]{:S(2)}) copy-start(f32[16,128,128]{2,1,0:T(8,128)} %get-tuple-element.15) | copy-start | bytes 3145732
  43.8 1.0 %copy-start.1 = (f32[432,128]{1,0:T(8,128)S(1)}, f32[432,128]{1,0:T(8,128)}, u32[]{:S(2)}) copy-start(f32[432,128]{1,0:T(8,128)} %get-tuple-element.28) | copy-start | bytes 663556

commit v3 on v2

--- a/solution.py
+++ b/solution.py
@@ -27,24 +27,29 @@
 
     lax.fori_loop(0, acc.shape[0], clear, 0)
 
-    def body(b, carry):
-        g = cot[b]
+    height = cot.shape[1]
+    both = 2
+
+    def body(i, carry):
+        g = jnp.concatenate([cot[i * both + h] for h in range(both)], axis=0)
         for k in range(0, offsets, 2):
             n = min(2, offsets - k)
             term = lax.dot_general(
                 g, w[k * cin : (k + n) * cin], (((1,), (1,)), ((), ())), preferred_element_type=F32
             )
-            for j in range(n):
-                source = block_map[b, k + j]
-                local = source - first
-                dead = jnp.logical_and(local - H >= live, local < slots + H)
-                skip = jnp.logical_or(jnp.logical_or(source < 0, b >= live), dead)
-                a = jnp.where(skip, nowhere, local)
-                idx[b, k + j] = a
-                acc[a] = acc[a] + term[:, j * cin : (j + 1) * cin]
+            for h in range(both):
+                b = i * both + h
+                for j in range(n):
+                    source = block_map[b, k + j]
+                    local = source - first
+                    dead = jnp.logical_and(local - H >= live, local < slots + H)
+                    skip = jnp.logical_or(jnp.logical_or(source < 0, b >= live), dead)
+                    a = jnp.where(skip, nowhere, local)
+                    idx[b, k + j] = a
+                    acc[a] = acc[a] + term[h * height : (h + 1) * height, j * cin : (j + 1) * cin]
         return carry
 
-    lax.fori_loop(0, slots, body, 0)
+    lax.fori_loop(0, slots // both, body, 0)
     for i in range(H):
         alive = jnp.where(slots - H + i < live, 1.0, 0.0).astype(BF16)
         top[i] = feat[slots - H + i] * alive
@@ -60,10 +65,10 @@
 
 def main_kernel(
     groups, space, unit, rows, padded,
-    idx, top, feat, w, cot, rims,
+    idx, top, feat, rims, w_far, cot_far,
     out, below, above, wg,
-    low, high, ext, turned, flat, part, r0, p1, r1, p2, r2, r3,
-    sh, qh, sr, qr, s0, q0, s1, q1, s2, q2, s3, q3,
+    w, cot, low, high, ext, turned, flat, part, r0, p1, r1, p2, r2, r3,
+    sl, sh, qh, sr, qr, s0, q0, s1, q1, s2, q2, s3, q3,
 ):
     g = lax.axis_index("grp")
     s = lax.axis_index("space")
@@ -90,11 +95,10 @@
         ext[i] = block
         turned[i] = block.T
 
-    for i in range(slots):
-        place(H + i, feat[i])
-    zero = jnp.zeros((height, cin), BF16)
-    for i in [2 * H + slots]:
-        place(i, zero)
+    load_cot = pltpu.make_async_copy(cot_far, cot, sl.at[0])
+    load_w = pltpu.make_async_copy(w_far, w, sl.at[1])
+    load_cot.start()
+    load_w.start()
     pl.semaphore_wait(barrier, len(fixed) + has_across.astype(jnp.int32))
 
     def remote(src, dst, send, recv, peer):
@@ -117,13 +121,10 @@
     def _():
         halo_up.start()
 
-    @pl.when(has_down)
-    def _():
-        down.start()
-
-    @pl.when(has_up)
-    def _():
-        up.start()
+    for i in range(slots):
+        place(H + i, feat[i])
+    zero = jnp.zeros((height, cin), BF16)
+    place(2 * H + slots, zero)
 
     @pl.when(has_down)
     def _():
@@ -147,6 +148,15 @@
         for i in range(H):
             place(H + slots + i, zero)
 
+    @pl.when(has_down)
+    def _():
+        down.start()
+
+    @pl.when(has_up)
+    def _():
+        up.start()
+
+    load_cot.wait()
     group = 3 if offsets % 3 == 0 else 1
     steps = offsets // group
     span = group * cin
@@ -160,7 +170,7 @@
         got = jnp.dot(jnp.concatenate(lhs, axis=0), cot[...], preferred_element_type=F32)
         at = pl.ds(pl.multiple_of(i * span, span), span)
         if direct:
-            part[at, :] = got.astype(BF16)
+            part[at, :] = got
         else:
             flat[at, :] = got
         return carry
@@ -185,8 +195,8 @@
         lax.fori_loop(0, steps, weight_step, 0)
         done = steps
         for p in range(space):
-            part[p * padded : p * padded + rows, :] = flat[p * rows : (p + 1) * rows, :].astype(BF16)
-            part[p * padded + rows : (p + 1) * padded, :] = jnp.zeros((padded - rows, part.shape[1]), BF16)
+            part[p * padded : p * padded + rows, :] = flat[p * rows : (p + 1) * rows, :]
+            part[p * padded + rows : (p + 1) * padded, :] = jnp.zeros((padded - rows, part.shape[1]), F32)
 
     here = window_start(g, groups, unit, padded)
     copies0, copies1 = [], []
@@ -201,11 +211,13 @@
             copies0[t].start()
         else:
             q = t - half
+            if q == 0:
+                load_w.wait()
             lax.fori_loop(q * pairs // 4, (q + 1) * pairs // 4, forward, 0)
         i = t - 1
         if 0 <= i < half:
             copies0[i].wait_recv()
-            p1[i] = (part[piece(2 * i + c), :].astype(F32) + r0[i].astype(F32)).astype(BF16)
+            p1[i] = (part[piece(2 * i + c), :] + r0[i]).astype(BF16)
             copies1.append([])
             for d in range(1, groups):
                 there = window_start((g + d) % groups, groups, unit, padded)
@@ -237,7 +249,7 @@
 
             for i in range(half):
                 total = total + r2[i].astype(F32)
-            r3[0] = total
+            r3[0] = total.astype(BF16)
             for d in range(1, groups):
                 copies3.append(remote(r3.at[0], r3.at[d], s3.at[d - 1], q3.at[d - 1], grp_peers[d - 1]))
                 copies3[-1].start()
@@ -246,7 +258,7 @@
         copy.wait_recv()
     for j in range(groups):
         at = min(j * unit, padded - unit)
-        wg[at : at + unit, :] = r3[(g - j + groups) % groups]
+        wg[at : at + unit, :] = r3[(g - j + groups) % groups].astype(F32)
 
     @pl.when(has_down)
     def _():
@@ -267,6 +279,21 @@
         @pl.when(z != i)
         def _(i=i):
             copies2[i].wait_send()
+
+
+def finish_kernel(space, where, counts, raw, own, below, above, wg_in, out, ig, wg):
+    slots = raw.shape[0]
+    device = where[0]
+    for i in range(slots):
+        alive = jnp.where(i < counts[0, 0], 1.0, 0.0).astype(F32)
+        value = own[i]
+        if i < H:
+            value = value + jnp.where(device > 0, below[i].astype(F32), 0.0)
+        if i >= slots - H:
+            value = value + jnp.where(device < space - 1, above[i - slots + H].astype(F32), 0.0)
+        ig[i] = (value * alive).astype(BF16)
+        out[i] = raw[i] * alive.astype(BF16)
+    wg[...] = wg_in[: wg.shape[0], :]
 
 
 def per_device(features, weights, cotangent, kernel_map, counts):
@@ -276,6 +303,7 @@
     space = lax.axis_size("space")
     groups = lax.axis_size("grp")
     device = lax.axis_index("space")
+    position = device.astype(jnp.int32).reshape(1)
     nowhere = slots + 2 * H
     flat_w = weights.reshape(offsets * cin, cout)
 
@@ -291,7 +319,7 @@
         out_specs=(SMEM, VMEM, VMEM, VMEM),
         scratch_shapes=[pltpu.VMEM((nowhere + 1, height, cin), F32)],
         name="input_grad",
-    )(device.astype(jnp.int32).reshape(1), counts, kernel_map[0], cotangent[0], voxels, flat_w)
+    )(position, counts, kernel_map[0], cotangent[0], voxels, flat_w)
 
     half = space // 2
     rows = offsets * cin // space
@@ -307,21 +335,24 @@
             rim,
             jax.ShapeDtypeStruct((padded, cout), F32),
         ),
-        in_specs=[SMEM] + [VMEM] * 5,
+        in_specs=[SMEM] + [VMEM] * 3 + [pl.BlockSpec(memory_space=pl.ANY)] * 2,
         out_specs=(VMEM,) * 4,
         scratch_shapes=[
+            pltpu.VMEM((offsets * cin, cout), BF16),
+            pltpu.VMEM((slots * height, cout), BF16),
             pltpu.VMEM((H, height, cin), BF16),
             pltpu.VMEM((H, height, cin), BF16),
             pltpu.VMEM((nowhere + 1, height, cin), BF16),
             pltpu.VMEM((nowhere + 1, cin, height), BF16),
             pltpu.VMEM((offsets * cin if rows != padded else 8, cout), F32),
-            pltpu.VMEM((space * padded, cout), BF16),
-            pltpu.VMEM((half, padded, cout), BF16),
+            pltpu.VMEM((space * padded, cout), F32),
+            pltpu.VMEM((half, padded, cout), F32),
             pltpu.VMEM((half, padded, cout), BF16),
             pltpu.VMEM((half, groups - 1, unit, cout), BF16),
             pltpu.VMEM((half, unit, cout), BF16),
             pltpu.VMEM((half, unit, cout), BF16),
-            pltpu.VMEM((groups, unit, cout), F32),
+            pltpu.VMEM((groups, unit, cout), BF16),
+            dma((2,)),
             dma((2,)), dma((2,)),
             dma((2,)), dma((2,)),
             dma((half,)), dma((half,)),
@@ -331,15 +362,19 @@
         ],
         compiler_params=pltpu.CompilerParams(collective_id=0, has_side_effects=True),
         name="main",
-    )(idx, top, voxels, flat_w, cotangent[0].reshape(slots * height, cout), rims)
-    alive = (jnp.arange(slots) < counts[0, 0])[:, None, None]
-    output = output * alive.astype(BF16)
-    below = jnp.where(device > 0, below.astype(F32), 0.0)
-    above = jnp.where(device < space - 1, above.astype(F32), 0.0)
-    gap = jnp.zeros((slots - H, height, cin), F32)
-    own = own + jnp.concatenate([below, gap], axis=0) + jnp.concatenate([gap, above], axis=0)
-    input_grad = (own * alive.astype(F32)).astype(BF16)
-    return output[None], input_grad[None], wg[:rows]
+    )(idx, top, voxels, rims, flat_w, cotangent[0].reshape(slots * height, cout))
+    output, input_grad, wg = pl.pallas_call(
+        functools.partial(finish_kernel, space),
+        out_shape=(
+            jax.ShapeDtypeStruct((slots, height, cout), BF16),
+            jax.ShapeDtypeStruct((slots, height, cin), BF16),
+            jax.ShapeDtypeStruct((rows, cout), F32),
+        ),
+        in_specs=[SMEM, SMEM] + [VMEM] * 5,
+        out_specs=(VMEM,) * 3,
+        name="finish",
+    )(position, counts, output, own, below, above, wg)
+    return output[None], input_grad[None], wg
 
 
 def solution(mesh):

time: 45.7 us -> 41.8 us (0.915)
  other arithmetic: 3.99 us -> 0 us
  Pallas kernels: 39.4 us -> 40.3 us
  local copies, waits for them, and re-layouts: 0.69 us -> 0 us
    broadcast_in_dim x2 -> x0, other arithmetic: 2.98 us -> none  [per_device(): return (output[None], input_grad[None], wg[:rows])]
    pallas_call x0 -> x1, Pallas kernels: none -> 2.65 us  [per_device(): pl.pallas_call(functools.partial(finish_kernel, space), out_shape=(jax.Sh...]
    pallas_call x1, Pallas kernels: 9.61 us -> 8.42 us  [per_device(): pl.pallas_call(input_grad_kernel, out_shape=(jax.ShapeDtypeStruct((slots,...]
    select_n x1 -> x0, other arithmetic: 1 us -> none  [per_device(): above = jnp.where(device < space - 1, above.astype(F32), 0.0)]
    unnamed x5 -> x0, local copies, waits for them, and re-layouts: 0.69 us -> none
    pallas_call x1, Pallas kernels: 29.8 us -> 29.2 us  [per_device(): pl.pallas_call(functools.partial(main_kernel, groups, space, unit, rows,...]
where the time goes in v3:
time: 41.8 us; the launch traced here: 41.6 us
  Pallas kernels  40.3 us (96%)
  between operations  1.3 us (3%)
    pallas_call x1, Pallas kernels, per_device(): pl.pallas_call(functools.partial(main_kernel, groups, space, unit, rows,...  29.2 us
    pallas_call x1, Pallas kernels, per_device(): pl.pallas_call(input_grad_kernel, out_shape=(jax.ShapeDtypeStruct((slots,...  8.42 us
    pallas_call x1, Pallas kernels, per_device(): pl.pallas_call(functools.partial(finish_kernel, space), out_shape=(jax.Sh...  2.65 us

profile of v3, /device:TPU:0, one launch (start us, length us, event | category | flops | bytes accessed | tf_op | source)
XLA Modules:
  0.0 41.6 jit_solution(7254801866755199652)
XLA Ops:
  1.3 8.4 %input_grad.1 = (s32[16,27]{1,0:T(8,128)}, bf16[4,128,128]{2,1,0:T(8,128)(2,1)}, bf16[2,4,128,128]{3,2,1,0:T(8,128)(2,1)}, f32[16,128,128]{2,1,0:T(8,128)}) custom-call(s32[1]{0:T(128)} %bitcast.where, s32[1,1]{1,0:T(1,128)S(6)} %copy.8.counts, s32[16,27]{1,0:T(8,128)} %bitcast.14, bf16[16,128,128]{2,1,0:T(8,128)(2,1)} %bitcast.10, ...), custom_call_target="tpu_custom_call" | custom-call | tf_op jit(solution)/shard_map/input_grad/pallas_call | solution.py:310
  9.7 29.2 %main.1 = (bf16[16,128,128]{2,1,0:T(8,128)(2,1)}, bf16[4,128,128]{2,1,0:T(8,128)(2,1)}, bf16[4,128,128]{2,1,0:T(8,128)(2,1)}, f32[432,128]{1,0:T(8,128)}) custom-call(s32[16,27]{1,0:T(8,128)} %get-tuple-element.14.idx, bf16[4,128,128]{2,1,0:T(8,128)(2,1)} %get-tuple-element.15.top, bf16[16,128,128]{2,1,0:T(8,128)(2,1)} %bitcast.13, ...), custom_call_target="tpu_custom_call" | custom-call | tf_op jit(solution)/shard_map/main/pallas_call | solution.py:330
  38.9 2.6 %finish.1 = (bf16[16,128,128]{2,1,0:T(8,128)(2,1)}, bf16[16,128,128]{2,1,0:T(8,128)(2,1)}, f32[432,128]{1,0:T(8,128)}) custom-call(s32[1]{0:T(128)} %bitcast.where, s32[1,1]{1,0:T(1,128)S(6)} %copy.8.counts, bf16[16,128,128]{2,1,0:T(8,128)(2,1)} %get-tuple-element.17.raw, f32[16,128,128]{2,1,0:T(8,128)} %get-tuple-element.18.own, ...), custom_call_target="tpu_custom_call" | custom-call | tf_op jit(solution)/shard_map/finish/pallas_call | solution.py:366

commit v4 on v3

--- a/solution.py
+++ b/solution.py
@@ -10,6 +10,7 @@
 H = 4
 BF16, F32 = jnp.bfloat16, jnp.float32
 VMEM = pl.BlockSpec(memory_space=pltpu.VMEM)
+FAR = pl.BlockSpec(memory_space=pl.ANY)
 SMEM = pl.BlockSpec(memory_space=pltpu.SMEM)
 
 
@@ -28,7 +29,7 @@
     lax.fori_loop(0, acc.shape[0], clear, 0)
 
     height = cot.shape[1]
-    both = 2
+    both = 4 if slots % 4 == 0 else 2
 
     def body(i, carry):
         g = jnp.concatenate([cot[i * both + h] for h in range(both)], axis=0)
@@ -67,7 +68,7 @@
     groups, space, unit, rows, padded,
     idx, top, feat, rims, w_far, cot_far,
     out, below, above, wg,
-    w, cot, low, high, ext, turned, flat, part, r0, p1, r1, p2, r2, r3,
+    w, cot, ext, turned, flat, part, r0, p1, r1, p2, r2, r3,
     sl, sh, qh, sr, qr, s0, q0, s1, q1, s2, q2, s3, q3,
 ):
     g = lax.axis_index("grp")
@@ -91,10 +92,11 @@
     def _():
         pl.semaphore_signal(barrier, inc=1, device_id=(g, across), device_id_type=pl.DeviceIdType.MESH)
 
-    def place(i, block):
-        ext[i] = block
-        turned[i] = block.T
-
+    def turn(i):
+        turned[i] = ext[i].T
+
+    load_feat = pltpu.make_async_copy(feat, ext.at[pl.ds(H, slots)], sl.at[2])
+    load_feat.start()
     load_cot = pltpu.make_async_copy(cot_far, cot, sl.at[0])
     load_w = pltpu.make_async_copy(w_far, w, sl.at[1])
     load_cot.start()
@@ -107,8 +109,8 @@
             device_id=peer, device_id_type=pl.DeviceIdType.MESH,
         )
 
-    halo_down = remote(feat.at[pl.ds(0, H)], high, sh.at[0], qh.at[0], (g, s - 1))
-    halo_up = remote(top, low, sh.at[1], qh.at[1], (g, s + 1))
+    halo_down = remote(feat.at[pl.ds(0, H)], ext.at[pl.ds(H + slots, H)], sh.at[0], qh.at[0], (g, s - 1))
+    halo_up = remote(top, ext.at[pl.ds(0, H)], sh.at[1], qh.at[1], (g, s + 1))
     down = remote(rims.at[0], above, sr.at[0], qr.at[0], (g, s - 1))
     up = remote(rims.at[1], below, sr.at[1], qr.at[1], (g, s + 1))
     has_down, has_up = s > 0, s < space - 1
@@ -121,32 +123,36 @@
     def _():
         halo_up.start()
 
+    zero = jnp.zeros((height, cin), BF16)
+    ext[2 * H + slots] = zero
+    turned[2 * H + slots] = zero
+    load_feat.wait()
     for i in range(slots):
-        place(H + i, feat[i])
-    zero = jnp.zeros((height, cin), BF16)
-    place(2 * H + slots, zero)
+        turn(H + i)
 
     @pl.when(has_down)
     def _():
         halo_up.wait_recv()
         for i in range(H):
-            place(i, low[i])
+            turn(i)
 
     @pl.when(jnp.logical_not(has_down))
     def _():
         for i in range(H):
-            place(i, zero)
+            ext[i] = zero
+            turned[i] = zero
 
     @pl.when(has_up)
     def _():
         halo_down.wait_recv()
         for i in range(H):
-            place(H + slots + i, high[i])
+            turn(H + slots + i)
 
     @pl.when(jnp.logical_not(has_up))
     def _():
         for i in range(H):
-            place(H + slots + i, zero)
+            ext[H + slots + i] = zero
+            turned[H + slots + i] = zero
 
     @pl.when(has_down)
     def _():
@@ -281,19 +287,52 @@
             copies2[i].wait_send()
 
 
-def finish_kernel(space, where, counts, raw, own, below, above, wg_in, out, ig, wg):
+def finish_kernel(
+    space, where, counts, raw_far, own_far, below_far, above_far, wg_far, out_far, ig_far, wg_out,
+    raw, own, below, above, wg_in, out, ig, wg, load, store,
+):
     slots = raw.shape[0]
     device = where[0]
-    for i in range(slots):
-        alive = jnp.where(i < counts[0, 0], 1.0, 0.0).astype(F32)
-        value = own[i]
-        if i < H:
-            value = value + jnp.where(device > 0, below[i].astype(F32), 0.0)
-        if i >= slots - H:
-            value = value + jnp.where(device < space - 1, above[i - slots + H].astype(F32), 0.0)
-        ig[i] = (value * alive).astype(BF16)
-        out[i] = raw[i] * alive.astype(BF16)
+    parts = slots // H
+    chunk = [pl.ds(q * H, H) for q in range(parts)]
+    copy = pltpu.make_async_copy
+    edges = [copy(below_far, below, load.at[2 * parts]), copy(above_far, above, load.at[2 * parts + 1])]
+    sums = copy(wg_far, wg_in, load.at[2 * parts + 2])
+    owns = [copy(own_far.at[chunk[q]], own.at[chunk[q]], load.at[q]) for q in range(parts)]
+    raws = [copy(raw_far.at[chunk[q]], raw.at[chunk[q]], load.at[parts + q]) for q in range(parts)]
+    for q in range(parts):
+        owns[q].start()
+        raws[q].start()
+        if q == 0:
+            for edge in edges:
+                edge.start()
+    sums.start()
+    stores = []
+    for q in range(parts):
+        owns[q].wait()
+        raws[q].wait()
+        if q == 0:
+            for edge in edges:
+                edge.wait()
+        for i in range(q * H, (q + 1) * H):
+            alive = jnp.where(i < counts[0, 0], 1.0, 0.0).astype(F32)
+            value = own[i]
+            if i < H:
+                value = value + jnp.where(device > 0, below[i].astype(F32), 0.0)
+            if i >= slots - H:
+                value = value + jnp.where(device < space - 1, above[i - slots + H].astype(F32), 0.0)
+            ig[i] = (value * alive).astype(BF16)
+            out[i] = raw[i] * alive.astype(BF16)
+        stores.append(copy(ig.at[chunk[q]], ig_far.at[chunk[q]], store.at[q]))
+        stores.append(copy(out.at[chunk[q]], out_far.at[chunk[q]], store.at[parts + q]))
+        stores[-2].start()
+        stores[-1].start()
+    sums.wait()
     wg[...] = wg_in[: wg.shape[0], :]
+    stores.append(copy(wg, wg_out, store.at[2 * parts]))
+    stores[-1].start()
+    for item in stores:
+        item.wait()
 
 
 def per_device(features, weights, cotangent, kernel_map, counts):
@@ -335,13 +374,11 @@
             rim,
             jax.ShapeDtypeStruct((padded, cout), F32),
         ),
-        in_specs=[SMEM] + [VMEM] * 3 + [pl.BlockSpec(memory_space=pl.ANY)] * 2,
+        in_specs=[SMEM] + [FAR] * 5,
         out_specs=(VMEM,) * 4,
         scratch_shapes=[
             pltpu.VMEM((offsets * cin, cout), BF16),
             pltpu.VMEM((slots * height, cout), BF16),
-            pltpu.VMEM((H, height, cin), BF16),
-            pltpu.VMEM((H, height, cin), BF16),
             pltpu.VMEM((nowhere + 1, height, cin), BF16),
             pltpu.VMEM((nowhere + 1, cin, height), BF16),
             pltpu.VMEM((offsets * cin if rows != padded else 8, cout), F32),
@@ -352,7 +389,7 @@
             pltpu.VMEM((half, unit, cout), BF16),
             pltpu.VMEM((half, unit, cout), BF16),
             pltpu.VMEM((groups, unit, cout), BF16),
-            dma((2,)),
+            dma((3,)),
             dma((2,)), dma((2,)),
             dma((2,)), dma((2,)),
             dma((half,)), dma((half,)),
@@ -370,8 +407,20 @@
             jax.ShapeDtypeStruct((slots, height, cin), BF16),
             jax.ShapeDtypeStruct((rows, cout), F32),
         ),
-        in_specs=[SMEM, SMEM] + [VMEM] * 5,
-        out_specs=(VMEM,) * 3,
+        in_specs=[SMEM, SMEM] + [FAR] * 5,
+        out_specs=(FAR,) * 3,
+        scratch_shapes=[
+            pltpu.VMEM((slots, height, cout), BF16),
+            pltpu.VMEM((slots, height, cin), F32),
+            pltpu.VMEM((H, height, cin), BF16),
+            pltpu.VMEM((H, height, cin), BF16),
+            pltpu.VMEM((padded, cout), F32),
+            pltpu.VMEM((slots, height, cout), BF16),
+            pltpu.VMEM((slots, height, cin), BF16),
+            pltpu.VMEM((rows, cout), F32),
+            dma((2 * (slots // H) + 3,)),
+            dma((2 * (slots // H) + 1,)),
+        ],
         name="finish",
     )(position, counts, output, own, below, above, wg)
     return output[None], input_grad[None], wg

time: 41.8 us -> 40.9 us (0.978)
  Pallas kernels: 40.3 us -> 39.4 us
    pallas_call x1, Pallas kernels: 8.42 us -> 7.76 us  [per_device(): pl.pallas_call(input_grad_kernel, out_shape=(jax.ShapeDtypeStruct((slots,...]
where the time goes in v4:
time: 40.9 us; the launch traced here: 40.6 us
  Pallas kernels  39.4 us (96%)
  between operations  1.3 us (3%)
    pallas_call x1, Pallas kernels, per_device(): pl.pallas_call(functools.partial(main_kernel, groups, space, unit, rows,...  29.1 us
    pallas_call x1, Pallas kernels, per_device(): pl.pallas_call(input_grad_kernel, out_shape=(jax.ShapeDtypeStruct((slots,...  7.76 us
    pallas_call x1, Pallas kernels, per_device(): pl.pallas_call(functools.partial(finish_kernel, space), out_shape=(jax.Sh...  2.45 us

profile of v4, /device:TPU:0, one launch (start us, length us, event | category | flops | bytes accessed | tf_op | source)
XLA Modules:
  0.0 40.6 jit_solution(2349839651449071921)
XLA Ops:
  1.3 7.8 %input_grad.1 = (s32[16,27]{1,0:T(8,128)}, bf16[4,128,128]{2,1,0:T(8,128)(2,1)}, bf16[2,4,128,128]{3,2,1,0:T(8,128)(2,1)}, f32[16,128,128]{2,1,0:T(8,128)}) custom-call(s32[1]{0:T(128)} %bitcast.where, s32[1,1]{1,0:T(1,128)S(6)} %copy.8.counts, s32[16,27]{1,0:T(8,128)} %bitcast.14, bf16[16,128,128]{2,1,0:T(8,128)(2,1)} %bitcast.10, ...), custom_call_target="tpu_custom_call" | custom-call | tf_op jit(solution)/shard_map/input_grad/pallas_call | solution.py:349
  9.0 29.1 %main.1 = (bf16[16,128,128]{2,1,0:T(8,128)(2,1)}, bf16[4,128,128]{2,1,0:T(8,128)(2,1)}, bf16[4,128,128]{2,1,0:T(8,128)(2,1)}, f32[432,128]{1,0:T(8,128)}) custom-call(s32[16,27]{1,0:T(8,128)} %get-tuple-element.14.idx, bf16[4,128,128]{2,1,0:T(8,128)(2,1)} %get-tuple-element.15.top, bf16[16,128,128]{2,1,0:T(8,128)(2,1)} %bitcast.13, ...), custom_call_target="tpu_custom_call" | custom-call | tf_op jit(solution)/shard_map/main/pallas_call | solution.py:369
  38.2 2.5 %finish.1 = (bf16[16,128,128]{2,1,0:T(8,128)(2,1)}, bf16[16,128,128]{2,1,0:T(8,128)(2,1)}, f32[432,128]{1,0:T(8,128)}) custom-call(s32[1]{0:T(128)} %bitcast.where, s32[1,1]{1,0:T(1,128)S(6)} %copy.8.counts, bf16[16,128,128]{2,1,0:T(8,128)(2,1)} %get-tuple-element.17.raw_far, f32[16,128,128]{2,1,0:T(8,128)} %get-tuple-element.18.own_far, ...), custom_call_target="tpu_custom_call" | custom-call | tf_op jit(solution)/shard_map/finish/pallas_call | solution.py:403
